TPU v7x, 32 devices: a whole 2x2x4 slice. The times are simulated.
32 devices in a mesh: row: 8 (over z, y), col: 4 (over x, core).
Axes of the slice: x: 2, y: 2, z: 4, core: 2. Of those that a mesh axis runs over, the one named last changes fastest.
Arguments:
- tokens_in: bfloat16 [192, 8192], P('row', 'col'), may hold values from -6 to 6
- gate_weight: bfloat16 [8192, 28672], P('col', 'row'), may hold values from -0.0625 to 0.0625
- up_weight: bfloat16 [8192, 28672], P('col', 'row'), may hold values from -0.0625 to 0.0625
- down_weight: bfloat16 [28672, 8192], P('row', 'col'), may hold values from -0.03125 to 0.03125
- out_grad: bfloat16 [192, 8192], P('row', 'col'), may hold values from -0.29882812 to 0.29882812
Outputs:
- output: bfloat16 [192, 8192], P('row', 'col')
- in_grad: bfloat16 [192, 8192], P('row', 'col')
- gate_grad: bfloat16 [8192, 28672], P('col', 'row')
- up_grad: bfloat16 [8192, 28672], P('col', 'row')
- down_grad: bfloat16 [28672, 8192], P('row', 'col')
All inputs are finite; a program needn't handle non-finite values.
Results may differ from a plain program's by a relative error of at most 0.0051.
Values may be sent and summed in bfloat16 or wider, within the bound.
A program may use at most 192 MiB of HBM per device.

v0:
```python
import jax
import jax.numpy as jnp
from jax import lax
from jax.sharding import PartitionSpec as P


def contract_last(left, right):
    return lax.dot_general(
        left, right, (((1,), (1,)), ((), ())), preferred_element_type=jnp.float32
    )


def contract_first(left, right):
    return lax.dot_general(
        left, right, (((0,), (0,)), ((), ())), preferred_element_type=jnp.float32
    )


def forward_gate(gate_pre, up_pre):
    sigma_gate = jax.nn.sigmoid(gate_pre)
    activated = gate_pre * sigma_gate
    hidden = (activated * up_pre).astype(jnp.bfloat16)
    return (hidden, sigma_gate, activated)


def backward_gate(d_hidden, gate_pre, up_pre, sigma_gate, activated):
    d_gate = (d_hidden * up_pre * sigma_gate * (1.0 + gate_pre * (1.0 - sigma_gate))).astype(
        jnp.bfloat16
    )
    d_up = (d_hidden * activated).astype(jnp.bfloat16)
    return (d_gate, d_up)


def shards(tokens_in, gate_weight, up_weight, down_weight, out_grad):
    inputs_all = lax.all_gather(tokens_in, "row", axis=0, tiled=True)
    gate_part = jnp.dot(inputs_all, gate_weight, preferred_element_type=jnp.float32)
    up_part = jnp.dot(inputs_all, up_weight, preferred_element_type=jnp.float32)
    gate_pre, up_pre = (
        lax.psum_scatter(gate_part, "col", scatter_dimension=0, tiled=True),
        lax.psum_scatter(up_part, "col", scatter_dimension=0, tiled=True),
    )
    hidden_share, sigma_gate, activated = forward_gate(gate_pre, up_pre)
    hidden_all = lax.all_gather(hidden_share, "col", axis=0, tiled=True)
    output = lax.psum_scatter(
        jnp.dot(hidden_all, down_weight, preferred_element_type=jnp.float32),
        "row",
        scatter_dimension=0,
        tiled=True,
    ).astype(jnp.bfloat16)
    grad_all = lax.all_gather(out_grad, "row", axis=0, tiled=True)
    dhid_part = contract_last(grad_all, down_weight)
    d_hidden = lax.psum_scatter(dhid_part, "col", scatter_dimension=0, tiled=True)
    d_gate, d_up = backward_gate(d_hidden, gate_pre, up_pre, sigma_gate, activated)
    d_gate_all, d_up_all = (
        lax.all_gather(d_gate, "col", axis=0, tiled=True),
        lax.all_gather(d_up, "col", axis=0, tiled=True),
    )
    in_grad = lax.psum_scatter(
        contract_last(d_gate_all, gate_weight) + contract_last(d_up_all, up_weight),
        "row",
        scatter_dimension=0,
        tiled=True,
    ).astype(jnp.bfloat16)
    gate_grad = contract_first(inputs_all, d_gate_all).astype(jnp.bfloat16)
    up_grad = contract_first(inputs_all, d_up_all).astype(jnp.bfloat16)
    down_grad = contract_first(hidden_all, grad_all).astype(jnp.bfloat16)
    return (output, in_grad, gate_grad, up_grad, down_grad)


def solution(mesh):
    in_specs = (P("row", "col"), P("col", "row"), P("col", "row"), P("row", "col"), P("row", "col"))
    out_specs = (
        P("row", "col"),
        P("row", "col"),
        P("col", "row"),
        P("col", "row"),
        P("row", "col"),
    )
    return jax.shard_map(shards, mesh=mesh, in_specs=in_specs, out_specs=out_specs, check_vma=False)
```

profile of v0, /device:TPU:0, one launch (start us, length us, event | category | flops | bytes accessed | tf_op | source)
XLA Modules:
  0.0 378.7 jit_solution(6762438291876996533)
XLA Ops:
  7.2 0.0 reduce-scatter.12.cloned.1.call-start
  7.2 34.1 %all_gather.17 = bf16[192,2048]{1,0:T(8,128)(2,1)S(1)} all-gather(bf16[24,2048]{1,0:T(8,128)(2,1)} %param.9), channel_id=1, replica_groups=mesh['row'=8,'col'=4] {'row'}, dimensions={0}, use_global_device_ids=true | all-gather | bytes 884736 | tf_op jit(solution)/shard_map/all_gather | solution.py:50
  41.3 11.7 %fusion.6 = f32[192,3584]{1,0:T(8,128)} fusion(bf16[192,2048]{1,0:T(8,128)(2,1)S(1)} %all_gather.17, bf16[3584,2048]{1,0:T(8,128)(2,1)} %param.8), kind=kOutput, calls=%fused_computation.14 | convolution fusion | flops 2818572288 | bytes 18219008 | tf_op jit(solution)/shard_map/dot_general | solution.py:8
  53.0 0.0 copy-start.3
  53.0 0.0 reduce-scatter.12.cloned.1.call-update
  53.0 0.0 reduce-scatter.6.cloned.1.call-start
  53.1 0.8 copy-done.3
  53.9 32.1 %all_gather.15 = bf16[192,2048]{1,0:T(8,128)(2,1)S(1)} all-gather(bf16[24,2048]{1,0:T(8,128)(2,1)S(1)} %copy-done.3), channel_id=1, replica_groups=mesh['row'=8,'col'=4] {'row'}, dimensions={0}, use_global_device_ids=true | all-gather | bytes 884736 | tf_op jit(solution)/shard_map/all_gather | solution.py:35
  86.0 9.8 %fusion.3 = f32[192,3584]{1,0:T(8,128)} fusion(bf16[192,2048]{1,0:T(8,128)(2,1)S(1)} %all_gather.15, bf16[2048,3584]{1,0:T(8,128)(2,1)} %param.6), kind=kOutput, calls=%fused_computation.11 | convolution fusion | flops 2818572288 | bytes 18219008 | tf_op jit(solution)/shard_map/dot_general | solution.py:36
  95.8 0.0 reduce-scatter.6.cloned.1.call-update
  95.8 0.0 reduce-scatter.8.cloned.1.call-start
  95.8 9.7 %fusion.4 = f32[192,3584]{1,0:T(8,128)} fusion(bf16[192,2048]{1,0:T(8,128)(2,1)S(1)} %all_gather.15, bf16[2048,3584]{1,0:T(8,128)(2,1)} %param.7), kind=kOutput, calls=%fused_computation.12 | convolution fusion | flops 2818572288 | bytes 18219008 | tf_op jit(solution)/shard_map/dot_general | solution.py:37
  105.5 0.0 reduce-scatter.8.cloned.1.call-update
  105.6 0.0 all-gather.4.cloned.1.call-start
  105.6 0.0 reduce-scatter.12.cloned.1.call-done
  105.6 26.5 %reduce-scatter.6.cloned.1.call-done = f32[48,3584]{1,0:T(8,128)} async-done(((f32[192,3584]{1,0:T(8,128)}), f32[48,3584]{1,0:T(8,128)}) %reduce-scatter.6.cloned.1.call-update) | async-done | bytes 688144 | tf_op jit(solution)/shard_map/reduce_scatter | solution.py:39
  132.1 38.5 %reduce-scatter.8.cloned.1.call-done = f32[48,3584]{1,0:T(8,128)} async-done(((f32[192,3584]{1,0:T(8,128)}), f32[48,3584]{1,0:T(8,128)}) %reduce-scatter.8.cloned.1.call-update) | async-done | bytes 688144 | tf_op jit(solution)/shard_map/reduce_scatter | solution.py:40
  170.7 2.8 multiply_convert_fusion
  173.4 0.0 all-gather.4.cloned.1.call-update
  173.5 0.0 all-gather.6.cloned.1.call-start
  173.5 0.5 all-gather.6.cloned.1.call-update
  174.1 0.0 all-gather.8.cloned.1.call-start
  174.1 0.5 all-gather.8.cloned.1.call-update
  174.6 0.0 reduce-scatter.10.cloned.1.call-start
  174.7 17.5 %all-gather.4.cloned.1.call-done = bf16[192,3584]{1,0:T(8,128)(2,1)} async-done(((bf16[48,3584]{1,0:T(8,128)(2,1)}), bf16[192,3584]{1,0:T(8,128)(2,1)}) %all-gather.4.cloned.1.call-update) | async-done | bytes 1376272 | tf_op jit(solution)/shard_map/all_gather | solution.py:43
  192.2 9.8 %fusion.5 = f32[192,2048]{1,0:T(8,128)} fusion(bf16[192,3584]{1,0:T(8,128)(2,1)} %all-gather.4.cloned.1.call-done, bf16[3584,2048]{1,0:T(8,128)(2,1)} %param.8), kind=kOutput, calls=%fused_computation.13 | convolution fusion | flops 2818572288 | bytes 17629184 | tf_op jit(solution)/shard_map/dot_general | solution.py:45
  201.9 0.0 reduce-scatter.10.cloned.1.call-update
  202.0 0.2 reduce-scatter.14.cloned.1.call-start
  202.2 10.5 %all-gather.6.cloned.1.call-done = bf16[192,3584]{1,0:T(8,128)(2,1)} async-done(((bf16[48,3584]{1,0:T(8,128)(2,1)}), bf16[192,3584]{1,0:T(8,128)(2,1)}) %all-gather.6.cloned.1.call-update) | async-done | bytes 1376272 | tf_op jit(solution)/shard_map/all_gather | solution.py:55
  212.7 8.5 %fusion.7 = f32[192,2048]{1,0:T(8,128)S(1)} fusion(bf16[192,3584]{1,0:T(8,128)(2,1)} %all-gather.6.cloned.1.call-done, bf16[2048,3584]{1,0:T(8,128)(2,1)} %param.6), kind=kOutput, calls=%fused_computation.15 | convolution fusion | flops 2818572288 | bytes 17629184 | tf_op jit(solution)/shard_map/dot_general | solution.py:8
  221.2 12.1 %all-gather.8.cloned.1.call-done = bf16[192,3584]{1,0:T(8,128)(2,1)} async-done(((bf16[48,3584]{1,0:T(8,128)(2,1)}), bf16[192,3584]{1,0:T(8,128)(2,1)}) %all-gather.8.cloned.1.call-update) | async-done | bytes 1376272 | tf_op jit(solution)/shard_map/all_gather | solution.py:56
  233.3 11.6 %convolution_add_fusion = f32[192,2048]{1,0:T(8,128)} fusion(f32[192,2048]{1,0:T(8,128)S(1)} %fusion.7, bf16[192,3584]{1,0:T(8,128)(2,1)} %all-gather.8.cloned.1.call-done, bf16[2048,3584]{1,0:T(8,128)(2,1)} %param.7), kind=kOutput, calls=%fused_computation.5 | convolution fusion | flops 2818965504 | bytes 19202048 | tf_op jit(solution)/shard_map/dot_general | solution.py:8
  244.9 0.0 copy-start.1
  244.9 0.0 reduce-scatter.14.cloned.1.call-update
  244.9 1.3 copy-done.1
  246.2 7.6 %fusion = bf16[2048,3584]{0,1:T(8,128)(2,1)} fusion(bf16[192,3584]{1,0:T(8,128)(2,1)S(1)} %copy-done.1, bf16[192,2048]{1,0:T(8,128)(2,1)S(1)} %all_gather.15), kind=kOutput, calls=%fused_computation.3 | convolution fusion | flops 2825912320 | bytes 16842752 | tf_op jit(solution)/shard_map/dot_general | solution.py:14
  253.8 0.0 copy-start.2
  253.8 18.8 %copy.10 = bf16[2048,3584]{1,0:T(8,128)(2,1)} copy(bf16[2048,3584]{0,1:T(8,128)(2,1)} %fusion) | data formatting | bytes 29360128
  272.6 0.0 copy-done.2
  272.6 7.6 %fusion.1 = bf16[2048,3584]{0,1:T(8,128)(2,1)} fusion(bf16[192,3584]{1,0:T(8,128)(2,1)S(1)} %copy-done.2, bf16[192,2048]{1,0:T(8,128)(2,1)S(1)} %all_gather.15), kind=kOutput, calls=%fused_computation.4 | convolution fusion | flops 2825912320 | bytes 16842752 | tf_op jit(solution)/shard_map/dot_general | solution.py:14
  280.2 0.0 copy-start
  280.2 18.8 %copy.11 = bf16[2048,3584]{1,0:T(8,128)(2,1)} copy(bf16[2048,3584]{0,1:T(8,128)(2,1)} %fusion.1) | data formatting | bytes 29360128
  299.0 0.0 copy-done
  299.0 7.6 %convolution_convert_fusion = bf16[3584,2048]{1,0:T(8,128)(2,1)} fusion(bf16[192,3584]{1,0:T(8,128)(2,1)S(1)} %copy-done, bf16[192,2048]{1,0:T(8,128)(2,1)S(1)} %all_gather.17), kind=kOutput, calls=%fused_computation | convolution fusion | flops 2825912320 | bytes 16842752 | tf_op jit(solution)/shard_map/dot_general | solution.py:14
  306.6 0.0 reduce-scatter.10.cloned.1.call-done
  306.6 1.6 convert_element_type.31
  308.2 62.1 %reduce-scatter.14.cloned.1.call-done = f32[24,2048]{1,0:T(8,128)} async-done(((f32[192,2048]{1,0:T(8,128)}), f32[24,2048]{1,0:T(8,128)}) %reduce-scatter.14.cloned.1.call-update) | async-done | bytes 196624 | tf_op jit(solution)/shard_map/reduce_scatter | solution.py:58
  370.3 1.6 convert_element_type.34
Async XLA Ops:
  7.2 98.5 %reduce-scatter.12.cloned.1.call-start = ((), (), s32[]{:S(2)}) async-start(), calls=%async_computation.9 | async-start | bytes 3440640 | tf_op jit(solution)/shard_map/reduce_scatter | solution.py:52
  53.0 0.9 copy-start.3
  53.0 79.1 %reduce-scatter.6.cloned.1.call-start = ((), (), s32[]{:S(2)}) async-start(), calls=%async_computation.5 | async-start | bytes 3440640 | tf_op jit(solution)/shard_map/reduce_scatter | solution.py:39
  95.8 74.9 %reduce-scatter.8.cloned.1.call-start = ((), (), s32[]{:S(2)}) async-start(), calls=%async_computation.6 | async-start | bytes 3440640 | tf_op jit(solution)/shard_map/reduce_scatter | solution.py:40
  105.6 86.6 %all-gather.4.cloned.1.call-start = ((), (), s32[]{:S(2)}) async-start(), calls=%async_computation.7 | async-start | bytes 1720320 | tf_op jit(solution)/shard_map/all_gather | solution.py:43
  173.5 39.2 %all-gather.6.cloned.1.call-start = ((), (), s32[]{:S(2)}) async-start(), calls=%async_computation.10 | async-start | bytes 1720320 | tf_op jit(solution)/shard_map/all_gather | solution.py:55
  174.1 59.2 %all-gather.8.cloned.1.call-start = ((), (), s32[]{:S(2)}) async-start(), calls=%async_computation.11 | async-start | bytes 1720320 | tf_op jit(solution)/shard_map/all_gather | solution.py:56
  174.6 132.0 %reduce-scatter.10.cloned.1.call-start = ((), (), s32[]{:S(2)}) async-start(), calls=%async_computation.8 | async-start | bytes 1769472 | tf_op jit(solution)/shard_map/reduce_scatter | solution.py:44
  202.0 168.3 %reduce-scatter.14.cloned.1.call-start = ((), (), s32[]{:S(2)}) async-start(), calls=%async_computation.12 | async-start | bytes 1769472 | tf_op jit(solution)/shard_map/reduce_scatter | solution.py:58
  244.9 1.3 copy-start.1
  253.8 18.8 %copy-start.2 = (bf16[192,3584]{1,0:T(8,128)(2,1)S(1)}, bf16[192,3584]{1,0:T(8,128)(2,1)}, u32[]{:S(2)}) copy-start(bf16[192,3584]{1,0:T(8,128)(2,1)} %all-gather.8.cloned.1.call-done) | copy-start | bytes 4128772
  280.2 18.8 %copy-start = (bf16[192,3584]{1,0:T(8,128)(2,1)S(1)}, bf16[192,3584]{1,0:T(8,128)(2,1)}, u32[]{:S(2)}) copy-start(bf16[192,3584]{1,0:T(8,128)(2,1)} %all-gather.4.cloned.1.call-done) | copy-start | bytes 4128772
Sparse Core Ops, SparseCore 0:
  53.1 36.2 reduce-scatter.11
  95.9 36.1 reduce-scatter.5
  135.3 35.3 reduce-scatter.7
  173.6 18.5 all-gather.3
  194.1 18.5 all-gather.5
  214.7 18.5 all-gather.7
  236.7 65.4 reduce-scatter.9
  305.6 64.6 reduce-scatter.13
where the time goes:
time: 380 us; the launch traced here: 379 us
  waiting for transfers between devices  168 us (44%)
  matrix products  83.8 us (22%)
  blocking collectives  66.2 us (17%)
  local copies, waits for them, and re-layouts  39.7 us (10%)
  between operations  14.2 us (4%)
  other arithmetic  5.93 us (2%)
    reduce_scatter x1, waiting for transfers between devices, shards(): lax.psum_scatter(contract_last(d_gate_all, gate_weight) + contract_last(d...  62.1 us
    unnamed x10, local copies, waits for them, and re-layouts  39.7 us
    reduce_scatter x1, waiting for transfers between devices, shards(): lax.psum_scatter(up_part, 'col', scatter_dimension=0, tiled=True)  38.5 us
    all_gather x1, blocking collectives, shards(): grad_all = lax.all_gather(out_grad, 'row', axis=0, tiled=True)  34.1 us
    all_gather x1, blocking collectives, shards(): inputs_all = lax.all_gather(tokens_in, 'row', axis=0, tiled=True)  32.1 us
    dot_general x3, matrix products, contract_last(): lax.dot_general(left, right, (((1,), (1,)), ((), ())), preferred_element_...  31.8 us
    reduce_scatter x1, waiting for transfers between devices, shards(): lax.psum_scatter(gate_part, 'col', scatter_dimension=0, tiled=True)  26.5 us
    dot_general x3, matrix products, contract_first(): lax.dot_general(left, right, (((0,), (0,)), ((), ())), preferred_element_...  22.8 us
  transfers between devices with their start and end apart: 8, of which 6 were waited for; matrix products, arithmetic and copies ran while one was open for 29% of the time, Pallas kernels for 0%

commit v1 on v0

--- a/solution.py
+++ b/solution.py
@@ -32,7 +32,8 @@
 
 
 def shards(tokens_in, gate_weight, up_weight, down_weight, out_grad):
-    inputs_all = lax.all_gather(tokens_in, "row", axis=0, tiled=True)
+    copies = jnp.concatenate([tokens_in] * lax.axis_size("row"), axis=0)
+    inputs_all = lax.all_to_all(copies, "row", 0, 0, tiled=True)
     gate_part = jnp.dot(inputs_all, gate_weight, preferred_element_type=jnp.float32)
     up_part = jnp.dot(inputs_all, up_weight, preferred_element_type=jnp.float32)
     gate_pre, up_pre = (

time: 380 us -> 375 us (0.987)
  waiting for transfers between devices: 168 us -> 212 us
  local copies, waits for them, and re-layouts: 39.7 us -> 0.9 us
  blocking collectives: 66.2 us -> 53.7 us
    unnamed x10 -> x15, local copies, waits for them, and re-layouts: 39.7 us -> 0.89 us
    reduce_scatter x1, waiting for transfers between devices: 0.01 us -> 34.2 us  [shards(): lax.psum_scatter(jnp.dot(hidden_all, down_weight, preferred_element_type=...]
    all_gather x1 -> x0, blocking collectives: 32.1 us -> none  [shards(): inputs_all = lax.all_gather(tokens_in, 'row', axis=0, tiled=True)]
    all_to_all x0 -> x1, blocking collectives: none -> 19.7 us  [shards(): inputs_all = lax.all_to_all(copies, 'row', 0, 0, tiled=True)]
    reduce_scatter x1, waiting for transfers between devices: 26.5 us -> 38.5 us  [shards(): lax.psum_scatter(gate_part, 'col', scatter_dimension=0, tiled=True)]
    reduce_scatter x1, waiting for transfers between devices: 62.1 us -> 66.4 us  [shards(): lax.psum_scatter(contract_last(d_gate_all, gate_weight) + contract_last(d...]
    reduce_scatter x1, waiting for transfers between devices: 38.5 us -> 34.6 us  [shards(): lax.psum_scatter(up_part, 'col', scatter_dimension=0, tiled=True)]
  transfers between devices with their start and end apart: 8 -> 8, of which waited for: 6 -> 7; matrix products, arithmetic and copies ran while one was open for 29% -> 21% of each run, Pallas kernels for 0% -> 0%
where the time goes in v1:
time: 375 us
  waiting for transfers between devices  212 us (57%)
  matrix products  87.5 us (23%)
  blocking collectives  53.7 us (14%)
  between operations  14.2 us (4%)
  other arithmetic  5.93 us (2%)
    reduce_scatter x1, waiting for transfers between devices, shards(): lax.psum_scatter(contract_last(d_gate_all, gate_weight) + contract_last(d...  66.4 us
    reduce_scatter x1, waiting for transfers between devices, shards(): lax.psum_scatter(gate_part, 'col', scatter_dimension=0, tiled=True)  38.5 us
    dot_general x3, matrix products, contract_last(): lax.dot_general(left, right, (((1,), (1,)), ((), ())), preferred_element_...  35.4 us
    reduce_scatter x1, waiting for transfers between devices, shards(): lax.psum_scatter(up_part, 'col', scatter_dimension=0, tiled=True)  34.6 us
    reduce_scatter x1, waiting for transfers between devices, shards(): lax.psum_scatter(jnp.dot(hidden_all, down_weight, preferred_element_type=...  34.2 us
    all_gather x1, blocking collectives, shards(): grad_all = lax.all_gather(out_grad, 'row', axis=0, tiled=True)  34.1 us
    dot_general x3, matrix products, contract_first(): lax.dot_general(left, right, (((0,), (0,)), ((), ())), preferred_element_...  22.8 us
    all_to_all x1, blocking collectives, shards(): inputs_all = lax.all_to_all(copies, 'row', 0, 0, tiled=True)  19.7 us
  transfers between devices with their start and end apart: 8, of which 7 were waited for; matrix products, arithmetic and copies ran while one was open for 21% of the time, Pallas kernels for 0%

profile of v1, /device:TPU:0, one launch (start us, length us, event | category | flops | bytes accessed | tf_op | source)
XLA Modules:
  0.0 374.6 jit_solution(9104480249063903465)
XLA Ops:
  7.2 0.0 reduce-scatter.12.cloned.1.call-start
  7.2 34.1 %all_gather.13 = bf16[192,2048]{1,0:T(8,128)(2,1)S(1)} all-gather(bf16[24,2048]{1,0:T(8,128)(2,1)} %param.9), channel_id=1, replica_groups=mesh['row'=8,'col'=4] {'row'}, dimensions={0}, use_global_device_ids=true | all-gather | bytes 884736 | tf_op jit(solution)/shard_map/all_gather | solution.py:51
  41.3 11.7 %fusion.4 = f32[192,3584]{1,0:T(8,128)} fusion(bf16[192,2048]{1,0:T(8,128)(2,1)S(1)} %all_gather.13, bf16[3584,2048]{1,0:T(8,128)(2,1)} %param.8), kind=kOutput, calls=%fused_computation.20 | convolution fusion | flops 2818572288 | bytes 18219008 | tf_op jit(solution)/shard_map/dot_general | solution.py:8
  53.0 0.0 copy-start
  53.0 0.0 reduce-scatter.12.cloned.1.call-update
  53.0 0.0 reduce-scatter.8.cloned.1.call-start
  53.1 0.8 copy-done
  54.0 19.7 %all_to_all.12 = bf16[8,24,2048]{2,1,0:T(8,128)(2,1)S(1)} all-to-all(bf16[8,24,2048]{2,1,0:T(8,128)(2,1)S(1)} %bitcast.24), channel_id=1, replica_groups=mesh['row'=8,'col'=4] {'row'}, dimensions={0} | all-to-all | bytes 1572864 | tf_op jit(solution)/shard_map/all_to_all | solution.py:36
  73.6 9.7 %fusion.2 = f32[192,3584]{1,0:T(8,128)} fusion(bf16[192,2048]{1,0:T(8,128)(2,1)S(1)} %bitcast.20, bf16[2048,3584]{1,0:T(8,128)(2,1)} %param.7), kind=kOutput, calls=%fused_computation.18 | convolution fusion | flops 2818572288 | bytes 18219008 | tf_op jit(solution)/shard_map/dot_general | solution.py:38
  83.4 0.0 reduce-scatter.8.cloned.1.call-update
  83.4 0.0 reduce-scatter.6.cloned.1.call-start
  83.4 9.8 %fusion.1 = f32[192,3584]{1,0:T(8,128)} fusion(bf16[192,2048]{1,0:T(8,128)(2,1)S(1)} %bitcast.21, bf16[2048,3584]{1,0:T(8,128)(2,1)} %param.6), kind=kOutput, calls=%fused_computation.17 | convolution fusion | flops 2818572288 | bytes 18219008 | tf_op jit(solution)/shard_map/dot_general | solution.py:37
  93.2 0.0 reduce-scatter.6.cloned.1.call-update
  93.2 0.0 all-gather.4.cloned.1.call-start
  93.3 0.0 reduce-scatter.12.cloned.1.call-done
  93.3 34.6 %reduce-scatter.8.cloned.1.call-done = f32[48,3584]{1,0:T(8,128)} async-done(((f32[192,3584]{1,0:T(8,128)}), f32[48,3584]{1,0:T(8,128)}) %reduce-scatter.8.cloned.1.call-update) | async-done | bytes 688144 | tf_op jit(solution)/shard_map/reduce_scatter | solution.py:41
  127.9 38.5 %reduce-scatter.6.cloned.1.call-done = f32[48,3584]{1,0:T(8,128)} async-done(((f32[192,3584]{1,0:T(8,128)}), f32[48,3584]{1,0:T(8,128)}) %reduce-scatter.6.cloned.1.call-update) | async-done | bytes 688144 | tf_op jit(solution)/shard_map/reduce_scatter | solution.py:40
  166.5 2.8 multiply_convert_fusion
  169.2 0.0 all-gather.4.cloned.1.call-update
  169.3 0.0 all-gather.6.cloned.1.call-start
  169.3 0.5 all-gather.6.cloned.1.call-update
  169.8 0.0 all-gather.8.cloned.1.call-start
  169.9 0.5 all-gather.8.cloned.1.call-update
  170.4 0.0 reduce-scatter.10.cloned.1.call-start
  170.5 17.5 %all-gather.4.cloned.1.call-done = bf16[192,3584]{1,0:T(8,128)(2,1)} async-done(((bf16[48,3584]{1,0:T(8,128)(2,1)}), bf16[192,3584]{1,0:T(8,128)(2,1)}) %all-gather.4.cloned.1.call-update) | async-done | bytes 1376272 | tf_op jit(solution)/shard_map/all_gather | solution.py:44
  187.9 9.8 %fusion.3 = f32[192,2048]{1,0:T(8,128)} fusion(bf16[192,3584]{1,0:T(8,128)(2,1)} %all-gather.4.cloned.1.call-done, bf16[3584,2048]{1,0:T(8,128)(2,1)} %param.8), kind=kOutput, calls=%fused_computation.19 | convolution fusion | flops 2818572288 | bytes 17629184 | tf_op jit(solution)/shard_map/dot_general | solution.py:46
  197.7 0.0 reduce-scatter.10.cloned.1.call-update
  197.7 0.2 reduce-scatter.14.cloned.1.call-start
  198.0 10.5 %all-gather.6.cloned.1.call-done = bf16[192,3584]{1,0:T(8,128)(2,1)} async-done(((bf16[48,3584]{1,0:T(8,128)(2,1)}), bf16[192,3584]{1,0:T(8,128)(2,1)}) %all-gather.6.cloned.1.call-update) | async-done | bytes 1376272 | tf_op jit(solution)/shard_map/all_gather | solution.py:56
  208.5 11.6 %fusion.5 = f32[192,2048]{1,0:T(8,128)} fusion(bf16[192,3584]{1,0:T(8,128)(2,1)} %all-gather.6.cloned.1.call-done, bf16[2048,3584]{1,0:T(8,128)(2,1)} %param.6), kind=kOutput, calls=%fused_computation.21 | convolution fusion | flops 2818572288 | bytes 17629184 | tf_op jit(solution)/shard_map/dot_general | solution.py:8
  220.1 8.9 %all-gather.8.cloned.1.call-done = bf16[192,3584]{1,0:T(8,128)(2,1)} async-done(((bf16[48,3584]{1,0:T(8,128)(2,1)}), bf16[192,3584]{1,0:T(8,128)(2,1)}) %all-gather.8.cloned.1.call-update) | async-done | bytes 1376272 | tf_op jit(solution)/shard_map/all_gather | solution.py:57
  229.0 0.0 copy-start.3
  229.0 12.1 %convolution_add_fusion = f32[192,2048]{1,0:T(8,128)} fusion(f32[192,2048]{1,0:T(8,128)} %fusion.5, bf16[192,3584]{1,0:T(8,128)(2,1)} %all-gather.8.cloned.1.call-done, bf16[2048,3584]{1,0:T(8,128)(2,1)} %param.7), kind=kOutput, calls=%fused_computation.3 | convolution fusion | flops 2818965504 | bytes 19202048 | tf_op jit(solution)/shard_map/dot_general | solution.py:8
  241.1 0.0 reduce-scatter.14.cloned.1.call-update
  241.2 0.0 copy-done.3
  241.2 0.0 copy-start.2
  241.2 7.6 %convolution_convert_fusion.1 = bf16[2048,3584]{1,0:T(8,128)(2,1)} fusion(bf16[192,2048]{1,0:T(8,128)(2,1)S(1)} %bitcast.22, bf16[192,3584]{1,0:T(8,128)(2,1)S(1)} %copy-done.3), kind=kOutput, calls=%fused_computation.1 | convolution fusion | flops 2825912320 | bytes 16842752 | tf_op jit(solution)/shard_map/dot_general | solution.py:14
  248.8 0.0 copy-done.2
  248.8 0.0 copy-start.1
  248.8 7.6 %convolution_convert_fusion.2 = bf16[2048,3584]{1,0:T(8,128)(2,1)} fusion(bf16[192,2048]{1,0:T(8,128)(2,1)S(1)} %bitcast.23, bf16[192,3584]{1,0:T(8,128)(2,1)S(1)} %copy-done.2), kind=kOutput, calls=%fused_computation.2 | convolution fusion | flops 2825912320 | bytes 16842752 | tf_op jit(solution)/shard_map/dot_general | solution.py:14
  256.4 0.0 copy-done.1
  256.4 7.6 %convolution_convert_fusion = bf16[3584,2048]{1,0:T(8,128)(2,1)} fusion(bf16[192,3584]{1,0:T(8,128)(2,1)S(1)} %copy-done.1, bf16[192,2048]{1,0:T(8,128)(2,1)S(1)} %all_gather.13), kind=kOutput, calls=%fused_computation | convolution fusion | flops 2825912320 | bytes 16842752 | tf_op jit(solution)/shard_map/dot_general | solution.py:14
  264.0 34.2 %reduce-scatter.10.cloned.1.call-done = f32[24,2048]{1,0:T(8,128)} async-done(((f32[192,2048]{1,0:T(8,128)}), f32[24,2048]{1,0:T(8,128)}) %reduce-scatter.10.cloned.1.call-update) | async-done | bytes 196624 | tf_op jit(solution)/shard_map/reduce_scatter | solution.py:45
  298.2 1.6 convert_element_type.25
  299.8 66.4 %reduce-scatter.14.cloned.1.call-done = f32[24,2048]{1,0:T(8,128)} async-done(((f32[192,2048]{1,0:T(8,128)}), f32[24,2048]{1,0:T(8,128)}) %reduce-scatter.14.cloned.1.call-update) | async-done | bytes 196624 | tf_op jit(solution)/shard_map/reduce_scatter | solution.py:59
  366.2 1.6 convert_element_type.28
  (8 shorter events, 0.1 us)
Async XLA Ops:
  7.2 86.1 %reduce-scatter.12.cloned.1.call-start = ((), (), s32[]{:S(2)}) async-start(), calls=%async_computation.10 | async-start | bytes 3440640 | tf_op jit(solution)/shard_map/reduce_scatter | solution.py:53
  53.0 0.9 copy-start
  53.0 74.9 %reduce-scatter.8.cloned.1.call-start = ((), (), s32[]{:S(2)}) async-start(), calls=%async_computation.7 | async-start | bytes 3440640 | tf_op jit(solution)/shard_map/reduce_scatter | solution.py:41
  83.4 83.1 %reduce-scatter.6.cloned.1.call-start = ((), (), s32[]{:S(2)}) async-start(), calls=%async_computation.6 | async-start | bytes 3440640 | tf_op jit(solution)/shard_map/reduce_scatter | solution.py:40
  93.2 94.7 %all-gather.4.cloned.1.call-start = ((), (), s32[]{:S(2)}) async-start(), calls=%async_computation.8 | async-start | bytes 1720320 | tf_op jit(solution)/shard_map/all_gather | solution.py:44
  169.3 39.2 %all-gather.6.cloned.1.call-start = ((), (), s32[]{:S(2)}) async-start(), calls=%async_computation.11 | async-start | bytes 1720320 | tf_op jit(solution)/shard_map/all_gather | solution.py:56
  169.8 59.2 %all-gather.8.cloned.1.call-start = ((), (), s32[]{:S(2)}) async-start(), calls=%async_computation.12 | async-start | bytes 1720320 | tf_op jit(solution)/shard_map/all_gather | solution.py:57
  170.4 127.8 %reduce-scatter.10.cloned.1.call-start = ((), (), s32[]{:S(2)}) async-start(), calls=%async_computation.9 | async-start | bytes 1769472 | tf_op jit(solution)/shard_map/reduce_scatter | solution.py:45
  197.7 168.4 %reduce-scatter.14.cloned.1.call-start = ((), (), s32[]{:S(2)}) async-start(), calls=%async_computation.13 | async-start | bytes 1769472 | tf_op jit(solution)/shard_map/reduce_scatter | solution.py:59
  229.0 12.1 %copy-start.3 = (bf16[192,3584]{1,0:T(8,128)(2,1)S(1)}, bf16[192,3584]{1,0:T(8,128)(2,1)}, u32[]{:S(2)}) copy-start(bf16[192,3584]{1,0:T(8,128)(2,1)} %all-gather.8.cloned.1.call-done) | copy-start | bytes 4128772
  241.2 7.6 %copy-start.2 = (bf16[192,3584]{1,0:T(8,128)(2,1)S(1)}, bf16[192,3584]{1,0:T(8,128)(2,1)}, u32[]{:S(2)}) copy-start(bf16[192,3584]{1,0:T(8,128)(2,1)} %all-gather.6.cloned.1.call-done) | copy-start | bytes 4128772
  248.8 7.6 %copy-start.1 = (bf16[192,3584]{1,0:T(8,128)(2,1)S(1)}, bf16[192,3584]{1,0:T(8,128)(2,1)}, u32[]{:S(2)}) copy-start(bf16[192,3584]{1,0:T(8,128)(2,1)} %all-gather.4.cloned.1.call-done) | copy-start | bytes 4128772
Sparse Core Ops, SparseCore 0:
  53.1 36.2 reduce-scatter.11
  92.6 35.3 reduce-scatter.7
  131.1 35.3 reduce-scatter.5
  169.4 18.5 all-gather.3
  189.9 18.5 all-gather.5
  210.5 18.5 all-gather.7
  232.5 65.7 reduce-scatter.9
  301.6 64.4 reduce-scatter.13
